TPU v7x, 32 devices: a whole 2x2x4 slice. The times are simulated.
32 devices in a mesh: cand: 8 (over y, x, core), ref: 4 (over z).
Axes of the slice: x: 2, y: 2, z: 4, core: 2. Of those that a mesh axis runs over, the one named last changes fastest.
Arguments:
- cand_factor: float32 [8192, 512], P('cand'), may hold values from -6 to 6
- ref_factor: float32 [2048, 512], P('ref'), may hold values from -6 to 6
- cand_plan: float32 [8192, 128], P('cand'), may hold values from 0.0625 to 16
- ref_plan: float32 [2048, 128], P('ref'), may hold values from 0.0625 to 16
- weights: float32 [128], replicated, may hold values from 0.5 to 2
Outputs:
- new_cand_plan: float32 [8192, 128], P('cand')
- new_ref_plan: float32 [2048, 128], P('ref')
- new_weights: float32 [128], replicated
All inputs are finite; a program needn't handle non-finite values. Where the computation divides by a largest or mean magnitude, that divisor is 1e-20 or more.
Results may differ from a plain program's by a relative error of at most 0.00019.
Values sent between devices are 32-bit elements; how exact they have to be, the bound alone decides.
No kernel may reach another device: no remote copies, remote signals or barrier semaphores. Data moves between devices by JAX's collectives and lax.ppermute only.
A program may use at most 64 MiB of HBM per device.

v0:
```python
import jax
import jax.numpy as jnp
from jax import lax
from jax.sharding import PartitionSpec as P

ITERS = 3
step_size = 3.0
tiny_value = 1e-06


def contract_rows(left, right):
    return lax.dot_general(
        left,
        right,
        (((0,), (0,)), ((), ())),
        precision=lax.Precision.HIGHEST,
        preferred_element_type=jnp.float32,
    )


def on_device(cand_factor, ref_factor, cand_plan, ref_plan, weights):
    cand_count = lax.axis_size("cand")
    ref_count = lax.axis_size("ref")
    cand_total = cand_factor.shape[0] * cand_count
    ref_total = ref_factor.shape[0] * ref_count
    rank_width = weights.shape[0]
    cand_block, cand_local = (cand_factor, cand_plan)
    ref_block, ref_local = (ref_factor, ref_plan)
    cand_partial = contract_rows(cand_block, cand_local) / cand_total
    ref_partial = contract_rows(ref_block, ref_local) / ref_total
    cand_moment = lax.psum(cand_partial, "cand")
    ref_moment = lax.psum(ref_partial, "ref")
    grad_cand = jnp.dot(cand_block, ref_moment, precision=lax.Precision.HIGHEST) / weights[None, :]
    grad_ref = jnp.dot(ref_block, cand_moment, precision=lax.Precision.HIGHEST) / weights[None, :]
    grad_weights = -jnp.sum(cand_moment * ref_moment, axis=0) / (weights * weights)
    local_top = jnp.maximum(jnp.max(jnp.abs(grad_cand)), jnp.max(jnp.abs(grad_ref)))
    global_top = lax.pmax(local_top, ("cand", "ref"))
    top = jnp.maximum(global_top, jnp.max(jnp.abs(grad_weights))) + tiny_value
    kernel_cand = cand_local * jnp.exp(-step_size * grad_cand / top)
    kernel_ref = ref_local * jnp.exp(-step_size * grad_ref / top)
    kernel_weights = weights * jnp.exp(-step_size * grad_weights / top)
    scale_cand = jnp.ones((rank_width,), jnp.float32)
    scale_ref = jnp.ones((rank_width,), jnp.float32)
    for repeat_index in range(ITERS):
        row_cand = rank_width / jnp.dot(kernel_cand, scale_cand, precision=lax.Precision.HIGHEST)
        row_ref = rank_width / jnp.dot(kernel_ref, scale_ref, precision=lax.Precision.HIGHEST)
        cand_mass_part = (
            jnp.dot(row_cand, kernel_cand, precision=lax.Precision.HIGHEST) / cand_total
        )
        ref_mass_part = jnp.dot(row_ref, kernel_ref, precision=lax.Precision.HIGHEST) / ref_total
        mass_cand = lax.psum(cand_mass_part, "cand")
        mass_ref = lax.psum(ref_mass_part, "ref")
        new_weights = jnp.cbrt(kernel_weights * scale_cand * mass_cand * scale_ref * mass_ref)
        scale_cand = new_weights / mass_cand
        scale_ref = new_weights / mass_ref
    new_cand_plan = row_cand[:, None] * kernel_cand * scale_cand[None, :]
    new_ref_plan = row_ref[:, None] * kernel_ref * scale_ref[None, :]
    return (new_cand_plan, new_ref_plan, new_weights)


def solution(mesh):
    in_specs = (P("cand", None), P("ref", None), P("cand", None), P("ref", None), P())
    out_specs = (P("cand", None), P("ref", None), P())
    return jax.shard_map(
        on_device, mesh=mesh, in_specs=in_specs, out_specs=out_specs, check_vma=False
    )
```

profile of v0, /device:TPU:0, one launch (start us, length us, event | category | flops | bytes accessed | tf_op | source)
XLA Modules:
  0.0 237.8 jit_solution(1407843614711286646)
XLA Ops:
  7.3 1.5 copy-done
  8.8 5.2 %convolution_multiply_fusion = f32[512,128]{1,0:T(8,128)} fusion(f32[1024,512]{1,0:T(8,128)S(1)} %copy-done, f32[1024,128]{1,0:T(8,128)} %param.7), kind=kOutput, calls=%fused_computation.1 | convolution fusion | flops 805371904 | bytes 2883584 | tf_op jit(solution)/shard_map/dot_general | solution.py:12
  14.0 2.5 %convolution_multiply_fusion.1 = f32[512,128]{1,0:T(8,128)} fusion(f32[512,512]{1,0:T(8,128)S(1)} %copy-done.1, f32[512,128]{1,0:T(8,128)S(1)} %copy-done.4), kind=kOutput, calls=%fused_computation.3 | convolution fusion | flops 402718720 | bytes 1572864 | tf_op jit(solution)/shard_map/dot_general | solution.py:12
  16.6 0.8 copy.9
  17.4 53.3 %all-reduce.5.cloned.1.call-done = f32[512,128]{1,0:T(8,128)} async-done(((f32[512,128]{1,0:T(8,128)}), f32[512,128]{1,0:T(8,128)}) %all-reduce.5.cloned.1.call-update) | async-done | bytes 262160 | tf_op jit(solution)/shard_map/psum | solution.py:31
  70.7 3.4 %abs_reduce_fusion.1 = (f32[]{:T(128)}, f32[128,512]{1,0:T(8,128)}) fusion(f32[128]{0:T(128)S(1)} %copy-done.5, f32[512,128]{1,0:T(8,128)} %all-reduce.5.cloned.1.call-done, f32[512,512]{1,0:T(8,128)S(1)} %copy-done.1), kind=kOutput, calls=%fused_computation.22 | convolution fusion | flops 402849792 | bytes 1573380 | tf_op jit(solution)/shard_map/dot_general | solution.py:34
  74.1 34.3 %all-reduce.3.cloned.1.call-done = f32[512,128]{1,0:T(8,128)} async-done(((f32[512,128]{1,0:T(8,128)}), f32[512,128]{1,0:T(8,128)}) %all-reduce.3.cloned.1.call-update) | async-done | bytes 262160 | tf_op jit(solution)/shard_map/psum | solution.py:32
  108.4 4.2 %abs_reduce_fusion = (f32[]{:T(128)}, f32[128,1024]{1,0:T(8,128)}) fusion(f32[128]{0:T(128)S(1)} %copy-done.5, f32[512,128]{1,0:T(8,128)} %all-reduce.3.cloned.1.call-done, f32[1024,512]{1,0:T(8,128)S(1)} %copy-done), kind=kOutput, calls=%fused_computation.18 | convolution fusion | flops 805699584 | bytes 2884100 | tf_op jit(solution)/shard_map/dot_general | solution.py:33
  114.2 40.2 %pmax.7 = f32[]{:T(128)} all-reduce(f32[]{:T(128)S(6)} %max.8), channel_id=1, replica_groups=mesh['cand'=8,'ref'=4] {'cand','ref'}, use_global_device_ids=true, to_apply=%region_4.0 | all-reduce | flops 1 | bytes 8 | tf_op jit(solution)/shard_map/pmax | solution.py:37
  154.4 1.0 multiply_reduce_fusion
  155.4 0.6 abs_reduce_fusion.2
  157.3 1.1 bitcast_multiply_fusion.1
  158.9 10.4 %psum.59 = f32[128]{0:T(128)S(1)} all-reduce(f32[128]{0:T(128)S(1)} %fusion), channel_id=1, replica_groups=mesh['cand'=8,'ref'=4] {'ref'}, use_global_device_ids=true, to_apply=%region_8.0 | all-reduce | flops 128 | bytes 1024 | tf_op jit(solution)/shard_map/psum | solution.py:52
  169.4 1.1 bitcast_multiply_fusion
  170.9 0.5 fusion.5
  171.4 11.8 %psum.58 = f32[128]{0:T(128)S(1)} all-reduce(f32[128]{0:T(128)S(1)} %fusion.5), channel_id=1, replica_groups=mesh['cand'=8,'ref'=4] {'cand'}, use_global_device_ids=true, to_apply=%region_7.0 | all-reduce | flops 128 | bytes 1024 | tf_op jit(solution)/shard_map/psum | solution.py:51
  184.2 8.4 %psum.61 = f32[128]{0:T(128)S(1)} all-reduce(f32[128]{0:T(128)S(1)} %fusion.1), channel_id=1, replica_groups=mesh['cand'=8,'ref'=4] {'ref'}, use_global_device_ids=true, to_apply=%region_10.0 | all-reduce | flops 128 | bytes 1024 | tf_op jit(solution)/shard_map/psum | solution.py:52
  192.6 0.5 fusion.4
  193.1 11.8 %psum.60 = f32[128]{0:T(128)S(1)} all-reduce(f32[128]{0:T(128)S(1)} %fusion.4), channel_id=1, replica_groups=mesh['cand'=8,'ref'=4] {'cand'}, use_global_device_ids=true, to_apply=%region_9.0 | all-reduce | flops 128 | bytes 1024 | tf_op jit(solution)/shard_map/psum | solution.py:51
  205.4 0.5 fusion.3
  205.9 12.1 %psum.62 = f32[128]{0:T(128)S(1)} all-reduce(f32[128]{0:T(128)S(1)} %fusion.3), channel_id=1, replica_groups=mesh['cand'=8,'ref'=4] {'cand'}, use_global_device_ids=true, to_apply=%region_11.0 | all-reduce | flops 128 | bytes 1024 | tf_op jit(solution)/shard_map/psum | solution.py:51
  218.5 10.4 %psum.63 = f32[128]{0:T(128)S(1)} all-reduce(f32[128]{0:T(128)S(1)} %fusion.2), channel_id=1, replica_groups=mesh['cand'=8,'ref'=4] {'ref'}, use_global_device_ids=true, to_apply=%region_12.0 | all-reduce | flops 128 | bytes 1024 | tf_op jit(solution)/shard_map/psum | solution.py:52
  229.0 0.8 copy.11
  230.0 1.0 copy.10
  (40 shorter events, 3.4 us)
Async XLA Ops:
  7.2 1.6 copy-start
  7.2 6.8 %copy-start.1 = (f32[512,512]{1,0:T(8,128)S(1)}, f32[512,512]{1,0:T(8,128)}, u32[]{:S(2)}) copy-start(f32[512,512]{1,0:T(8,128)} %param.6) | copy-start | bytes 3145732
  7.2 6.8 %copy-start.4 = (f32[512,128]{1,0:T(8,128)S(1)}, f32[512,128]{1,0:T(8,128)}, u32[]{:S(2)}) copy-start(f32[512,128]{1,0:T(8,128)} %param.8) | copy-start | bytes 786436
  7.2 63.5 %copy-start.5 = (f32[128]{0:T(128)S(1)}, f32[128]{0:T(128)}, u32[]{:S(2)}) copy-start(f32[128]{0:T(128)} %param.9) | copy-start | bytes 1540
  7.2 63.5 %all-reduce.5.cloned.1.call-start = ((), (), s32[]{:S(2)}) async-start(), calls=%async_computation.1 | async-start | bytes 524288 | tf_op jit(solution)/shard_map/psum | solution.py:31
  14.0 94.5 %all-reduce.3.cloned.1.call-start = ((), (), s32[]{:S(2)}) async-start(), calls=%async_computation | async-start | bytes 524288 | tf_op jit(solution)/shard_map/psum | solution.py:32
  74.1 39.9 %copy-start.2 = (f32[1024,128]{1,0:T(8,128)S(1)}, f32[1024,128]{1,0:T(8,128)}, u32[]{:S(2)}) copy-start(f32[1024,128]{1,0:T(8,128)} %param.7) | copy-start | bytes 1572868
  74.1 80.3 %copy-start.3 = (f32[512,128]{1,0:T(8,128)S(1)}, f32[512,128]{1,0:T(8,128)}, u32[]{:S(2)}) copy-start(f32[512,128]{1,0:T(8,128)} %all-reduce.5.cloned.1.call-done) | copy-start | bytes 786436
  228.9 2.1 copy-start.6
Sparse Core Ops, SparseCore 0:
  14.1 56.5 all-reduce.4
  73.6 34.7 all-reduce.2
where the time goes:
time: 238 us
  blocking collectives  105 us (44%)
  waiting for transfers between devices  87.7 us (37%)
  matrix products  19.6 us (8%)
  between operations  16.8 us (7%)
  local copies, waits for them, and re-layouts  4.4 us (2%)
  other arithmetic  4.18 us (2%)
    psum x1, waiting for transfers between devices, on_device(): cand_moment = lax.psum(cand_partial, 'cand')  53.3 us
    pmax x1, blocking collectives, on_device(): global_top = lax.pmax(local_top, ('cand', 'ref'))  40.2 us
    psum x3, blocking collectives, on_device(): mass_cand = lax.psum(cand_mass_part, 'cand')  35.7 us
    psum x1, waiting for transfers between devices, on_device(): ref_moment = lax.psum(ref_partial, 'ref')  34.3 us
    psum x3, blocking collectives, on_device(): mass_ref = lax.psum(ref_mass_part, 'ref')  29.3 us
    dot_general x2, matrix products, contract_rows(): lax.dot_general(left, right, (((0,), (0,)), ((), ())), precision=lax.Prec...  7.68 us
  transfers between devices with their start and end apart: 2, of which 2 were waited for; matrix products, arithmetic and copies ran while one was open for 3% of the time, Pallas kernels for 0%

commit v1 on v0

--- a/solution.py
+++ b/solution.py
@@ -28,7 +28,7 @@
     ref_block, ref_local = (ref_factor, ref_plan)
     cand_partial = contract_rows(cand_block, cand_local) / cand_total
     ref_partial = contract_rows(ref_block, ref_local) / ref_total
-    cand_moment = lax.psum(cand_partial, "cand")
+    cand_moment = jnp.sum(lax.all_gather(cand_partial, "cand"), axis=0)
     ref_moment = lax.psum(ref_partial, "ref")
     grad_cand = jnp.dot(cand_block, ref_moment, precision=lax.Precision.HIGHEST) / weights[None, :]
     grad_ref = jnp.dot(ref_block, cand_moment, precision=lax.Precision.HIGHEST) / weights[None, :]

time: 238 us -> 185 us (0.78)
  waiting for transfers between devices: 87.7 us -> 32.4 us
    psum x1 -> x0, waiting for transfers between devices: 53.3 us -> none  [on_device(): cand_moment = lax.psum(cand_partial, 'cand')]
  transfers between devices with their start and end apart: 2 -> 2, of which waited for: 2 -> 1; matrix products, arithmetic and copies ran while one was open for 3% -> 6% of each run, Pallas kernels for 0% -> 0%
where the time goes in v1:
time: 185 us; the launch traced here: 184 us
  blocking collectives  105 us (57%)
  waiting for transfers between devices  32.4 us (18%)
  matrix products  19 us (10%)
  between operations  18.2 us (10%)
  other arithmetic  6.07 us (3%)
  local copies, waits for them, and re-layouts  3.71 us (2%)
    pmax x1, blocking collectives, on_device(): global_top = lax.pmax(local_top, ('cand', 'ref'))  40.2 us
    psum x3, blocking collectives, on_device(): mass_cand = lax.psum(cand_mass_part, 'cand')  35.4 us
    psum x1, waiting for transfers between devices, on_device(): ref_moment = lax.psum(ref_partial, 'ref')  32.4 us
    psum x3, blocking collectives, on_device(): mass_ref = lax.psum(ref_mass_part, 'ref')  29.2 us
    dot_general x2, matrix products, contract_rows(): lax.dot_general(left, right, (((0,), (0,)), ((), ())), precision=lax.Prec...  8.07 us
    dot_general x1, matrix products, on_device(): jnp.dot(cand_block, ref_moment, precision=lax.Precision.HIGHEST)  4.22 us
    unnamed x16, local copies, waits for them, and re-layouts  3.71 us
  transfers between devices with their start and end apart: 2, of which 1 were waited for; matrix products, arithmetic and copies ran while one was open for 6% of the time, Pallas kernels for 0%

profile of v1, /device:TPU:0, one launch (start us, length us, event | category | flops | bytes accessed | tf_op | source)
XLA Modules:
  0.0 184.2 jit_solution(7872237270090756091)
XLA Ops:
  8.1 3.9 %convolution_multiply_fusion.1 = f32[512,128]{1,0:T(8,128)} fusion(f32[512,512]{1,0:T(8,128)} %param.6, f32[512,128]{1,0:T(8,128)} %param.8), kind=kOutput, calls=%fused_computation.3 | convolution fusion | flops 402718720 | bytes 1572864 | tf_op jit(solution)/shard_map/dot_general | solution.py:12
  12.1 4.1 %convolution_multiply_fusion = f32[512,128]{1,0:T(8,128)} fusion(f32[1024,512]{1,0:T(8,128)S(1)} %copy-done, f32[1024,128]{1,0:T(8,128)S(1)} %copy-done.2), kind=kOutput, calls=%fused_computation.1 | convolution fusion | flops 805371904 | bytes 2883584 | tf_op jit(solution)/shard_map/dot_general | solution.py:12
  16.3 0.9 copy.9
  17.1 1.0 copy.8
  18.1 32.4 %all-reduce.2.cloned.1.call-done = f32[512,128]{1,0:T(8,128)} async-done(((f32[512,128]{1,0:T(8,128)}), f32[512,128]{1,0:T(8,128)}) %all-reduce.2.cloned.1.call-update) | async-done | bytes 262160 | tf_op jit(solution)/shard_map/psum | solution.py:32
  50.5 4.2 %abs_reduce_fusion = (f32[]{:T(128)}, f32[128,1024]{1,0:T(8,128)}) fusion(f32[128]{0:T(128)S(1)} %copy-done.4, f32[512,128]{1,0:T(8,128)} %all-reduce.2.cloned.1.call-done, f32[1024,512]{1,0:T(8,128)S(1)} %copy-done), kind=kOutput, calls=%fused_computation.18 | convolution fusion | flops 805699584 | bytes 2884100 | tf_op jit(solution)/shard_map/dot_general | solution.py:33
  54.7 1.7 reduce_sum.18
  56.5 2.4 %abs_reduce_fusion.1 = (f32[]{:T(128)}, f32[128,512]{1,0:T(8,128)}) fusion(f32[128]{0:T(128)S(1)} %copy-done.4, f32[512,128]{1,0:T(8,128)S(1)} %reduce_sum.18, f32[512,512]{1,0:T(8,128)S(1)} %copy-done.1), kind=kOutput, calls=%fused_computation.22 | convolution fusion | flops 402849792 | bytes 1573380 | tf_op jit(solution)/shard_map/dot_general | solution.py:34
  60.2 1.0 multiply_reduce_fusion
  61.2 0.6 abs_reduce_fusion.2
  61.9 40.2 %pmax.7 = f32[]{:T(128)} all-reduce(f32[]{:T(128)S(6)} %max.8), channel_id=1, replica_groups=mesh['cand'=8,'ref'=4] {'cand','ref'}, use_global_device_ids=true, to_apply=%region_4.0 | all-reduce | flops 1 | bytes 8 | tf_op jit(solution)/shard_map/pmax | solution.py:37
  103.3 1.1 bitcast_multiply_fusion.1
  104.9 10.4 %psum.51 = f32[128]{0:T(128)S(1)} all-reduce(f32[128]{0:T(128)S(1)} %fusion), channel_id=1, replica_groups=mesh['cand'=8,'ref'=4] {'ref'}, use_global_device_ids=true, to_apply=%region_8.0 | all-reduce | flops 128 | bytes 1024 | tf_op jit(solution)/shard_map/psum | solution.py:52
  115.3 1.3 bitcast_multiply_fusion
  117.0 0.5 fusion.5
  117.5 11.8 %psum.50 = f32[128]{0:T(128)S(1)} all-reduce(f32[128]{0:T(128)S(1)} %fusion.5), channel_id=1, replica_groups=mesh['cand'=8,'ref'=4] {'cand'}, use_global_device_ids=true, to_apply=%region_7.0 | all-reduce | flops 128 | bytes 1024 | tf_op jit(solution)/shard_map/psum | solution.py:51
  130.3 8.4 %psum.53 = f32[128]{0:T(128)S(1)} all-reduce(f32[128]{0:T(128)S(1)} %fusion.1), channel_id=1, replica_groups=mesh['cand'=8,'ref'=4] {'ref'}, use_global_device_ids=true, to_apply=%region_10.0 | all-reduce | flops 128 | bytes 1024 | tf_op jit(solution)/shard_map/psum | solution.py:52
  138.7 0.5 fusion.4
  139.2 11.8 %psum.52 = f32[128]{0:T(128)S(1)} all-reduce(f32[128]{0:T(128)S(1)} %fusion.4), channel_id=1, replica_groups=mesh['cand'=8,'ref'=4] {'cand'}, use_global_device_ids=true, to_apply=%region_9.0 | all-reduce | flops 128 | bytes 1024 | tf_op jit(solution)/shard_map/psum | solution.py:51
  151.6 10.4 %psum.55 = f32[128]{0:T(128)S(1)} all-reduce(f32[128]{0:T(128)S(1)} %fusion.2), channel_id=1, replica_groups=mesh['cand'=8,'ref'=4] {'ref'}, use_global_device_ids=true, to_apply=%region_12.0 | all-reduce | flops 128 | bytes 1024 | tf_op jit(solution)/shard_map/psum | solution.py:52
  162.4 0.5 fusion.3
  162.9 11.8 %psum.54 = f32[128]{0:T(128)S(1)} all-reduce(f32[128]{0:T(128)S(1)} %fusion.3), channel_id=1, replica_groups=mesh['cand'=8,'ref'=4] {'cand'}, use_global_device_ids=true, to_apply=%region_11.0 | all-reduce | flops 128 | bytes 1024 | tf_op jit(solution)/shard_map/psum | solution.py:51
  174.9 0.8 copy.11
  175.8 1.0 copy.10
  (39 shorter events, 3.2 us)
Async XLA Ops:
  8.0 4.1 %copy-start = (f32[1024,512]{1,0:T(8,128)S(1)}, f32[1024,512]{1,0:T(8,128)}, u32[]{:S(2)}) copy-start(f32[1024,512]{1,0:T(8,128)} %param.5) | copy-start | bytes 6291460
  8.0 4.1 %copy-start.2 = (f32[1024,128]{1,0:T(8,128)S(1)}, f32[1024,128]{1,0:T(8,128)}, u32[]{:S(2)}) copy-start(f32[1024,128]{1,0:T(8,128)} %param.7) | copy-start | bytes 1572868
  8.0 42.5 %all-reduce.2.cloned.1.call-start = ((), (), s32[]{:S(2)}) async-start(), calls=%async_computation | async-start | bytes 524288 | tf_op jit(solution)/shard_map/psum | solution.py:32
  12.0 4.3 %copy-start.3 = (f32[512,128]{1,0:T(8,128)S(1)}, f32[512,128]{1,0:T(8,128)}, u32[]{:S(2)}) copy-start(f32[512,128]{1,0:T(8,128)} %param.8) | copy-start | bytes 786436
  12.0 38.5 %copy-start.4 = (f32[128]{0:T(128)S(1)}, f32[128]{0:T(128)}, u32[]{:S(2)}) copy-start(f32[128]{0:T(128)} %param.9) | copy-start | bytes 1540
  12.0 42.7 %all-gather.3.cloned.1.call-start = ((), (), s32[]{:S(2)}) async-start(), calls=%async_computation.1 | async-start | bytes 2359296 | tf_op jit(solution)/shard_map/all_gather | solution.py:31
  18.1 38.3 %copy-start.1 = (f32[512,512]{1,0:T(8,128)S(1)}, f32[512,512]{1,0:T(8,128)}, u32[]{:S(2)}) copy-start(f32[512,512]{1,0:T(8,128)} %param.6) | copy-start | bytes 3145732
  174.7 2.1 %copy-start.5 = (f32[128]{0:T(128)}, f32[128]{0:T(128)S(1)}, u32[]{:S(2)}) copy-start(f32[128]{0:T(128)S(1)} %get-tuple-element.7) | copy-start | bytes 1540
Sparse Core Ops, SparseCore 0:
  12.1 38.3 all-reduce.1
Sparse Core Ops, SparseCore 1:
  16.4 30.4 all-gather.2
